TPU v7x, 128 devices: a whole 4x4x4 slice. The times are simulated.
128 devices in a mesh: node: 32 (over z, y_lo, x), rep: 4 (over y_hi, core).
Axes of the slice: x: 4, y: 4 (y_hi: 2, y_lo: 2; y = y_hi * 2 + y_lo), z: 4, core: 2. Of those that a mesh axis runs over, the one named last changes fastest.
Arguments:
- node_feats: bfloat16 [65536, 256], P('node'), may hold values from -6 to 6
- weight: bfloat16 [256, 256], replicated, may hold values from -0.375 to 0.375
- cotangent: bfloat16 [65536, 256], P(('node', 'rep')), may hold values from -6 to 6
- tiles: bfloat16 [32, 4, 160, 256, 256], P('node', 'rep'), may hold values from -0.049804688 to 0.049804688
- tile_rows: int32 [32, 4, 160], P('node', 'rep'), may hold values from 0 to 7
- tile_cols: int32 [32, 4, 160], P('node', 'rep'), may hold values from 0 to 63
- tile_count: int32 [32, 4], P('node', 'rep'), may hold values from 80 to 160, as said below
Outputs:
- activated: bfloat16 [65536, 256], P(('node', 'rep'))
- feature_grad: bfloat16 [65536, 256], P(('node', 'rep'))
- weight_grad: float32 [256, 256], replicated
Inputs may be any that keep to these rules, and one draw needn't show every extreme that they name: `tile_count`: slots at and beyond a device's count are ignored; some device has all 160 slots live in every draw.
All inputs are finite; a program needn't handle non-finite values.
Results may differ from a plain program's by a relative error of at most 0.007.
Values may be sent and summed in bfloat16 or wider, within the bound.
No kernel may reach another device: no remote copies, remote signals or barrier semaphores. Data moves between devices by JAX's collectives and lax.ppermute only.
A program may use at most 256 MiB of HBM per device.

v0:
```python
import jax
import jax.numpy as jnp
from jax import lax
from jax.sharding import PartitionSpec as P


def body(node_feats, weight, cotangent, tiles, tile_rows, tile_cols, tile_count):
    nrep = lax.axis_size("rep")
    nnode = lax.axis_size("node")
    rep_idx = lax.axis_index("rep")
    rows, feat = node_feats.shape
    block = tiles.shape[-1]
    row_blocks = rows // block
    quarter = row_blocks // nrep
    share = rows // nrep
    compact_cols = quarter * nnode
    slot_tiles = tiles[0, 0]
    slot_rows = tile_rows[0, 0]
    slot_cols = tile_cols[0, 0]
    slot_total = slot_tiles.shape[0]
    live = jnp.arange(slot_total, dtype=jnp.int32) < tile_count[0, 0]
    live_scale = live.astype(jnp.float32)[:, None, None]
    feat_blocks = node_feats.reshape(row_blocks, block, feat)
    mine = lax.dynamic_slice_in_dim(feat_blocks, rep_idx * quarter, quarter, 0)
    compact = lax.all_gather(mine, "node", axis=0, tiled=True)
    picked = compact[slot_cols]
    forward_prod = (
        jnp.einsum("tab,tbf->taf", slot_tiles, picked, preferred_element_type=jnp.float32)
        * live_scale
    )
    partial_agg = (
        jnp.zeros((row_blocks, block, feat), jnp.float32)
        .at[slot_rows]
        .add(forward_prod)
        .reshape(rows, feat)
    )
    scale = float(rows * nnode) ** (-0.5)
    aggregated = lax.psum(partial_agg, "rep").astype(jnp.bfloat16)
    cot_full = lax.all_gather(cotangent, "rep", axis=0, tiled=True)
    pre = jnp.dot(aggregated, weight, preferred_element_type=jnp.float32)
    sig = jax.nn.sigmoid(pre)
    activated_full = (pre * sig).astype(jnp.bfloat16)
    dpre = (cot_full.astype(jnp.float32) * sig * (1.0 + pre * (1.0 - sig))).astype(jnp.bfloat16)
    dagg = jnp.dot(dpre, weight.T, preferred_element_type=jnp.float32).astype(jnp.bfloat16)
    activated = lax.dynamic_slice_in_dim(activated_full, rep_idx * share, share, 0)
    agg_share = lax.dynamic_slice_in_dim(aggregated, rep_idx * share, share, 0)
    dpre_share = lax.dynamic_slice_in_dim(dpre, rep_idx * share, share, 0)
    weight_term = lax.dot_general(
        agg_share, dpre_share, (((0,), (0,)), ((), ())), preferred_element_type=jnp.float32
    )
    weight_grad = lax.psum(weight_term, ("node", "rep")) * scale
    dagg_blocks = dagg.reshape(row_blocks, block, feat)
    backward_prod = (
        jnp.einsum(
            "tab,taf->tbf", slot_tiles, dagg_blocks[slot_rows], preferred_element_type=jnp.float32
        )
        * live_scale
    )
    column_part = (
        jnp.zeros((compact_cols, block, feat), jnp.float32).at[slot_cols].add(backward_prod)
    )
    owned = lax.psum_scatter(column_part, "node", scatter_dimension=0, tiled=True)
    feature_grad = owned.reshape(quarter * block, feat).astype(jnp.bfloat16)
    return (activated, feature_grad, weight_grad)


def solution(mesh):
    placed = (
        P("node", None),
        P(),
        P(("node", "rep"), None),
        P("node", "rep", None, None, None),
        P("node", "rep", None),
        P("node", "rep", None),
        P("node", "rep"),
    )
    return jax.shard_map(
        body,
        mesh=mesh,
        in_specs=placed,
        out_specs=(P(("node", "rep"), None), P(("node", "rep"), None), P()),
        check_vma=False,
    )
```

profile of v0, /device:TPU:0, one launch (start us, length us, event | category | flops | bytes accessed | tf_op | source)
XLA Modules:
  0.0 760.6 jit_solution(5284792371590088112)
XLA Ops:
  7.2 1.2 copy-done
  8.4 0.7 constant_dynamic-slice_fusion
  9.2 0.7 all-gather.5.cloned.1.call-update
  9.9 0.7 compare_select_fusion
  11.3 0.7 compare_select_fusion.1
  12.0 167.9 %all-gather.3.cloned.1.call-done = bf16[64,256,256]{2,1,0:T(8,128)(2,1)} async-done(((bf16[2,256,256]{2,1,0:T(8,128)(2,1)}), bf16[64,256,256]{2,1,0:T(8,128)(2,1)}) %all-gather.3.cloned.1.call-update) | async-done | bytes 8388624 | tf_op jit(solution)/shard_map/all_gather | solution.py:25
  179.9 13.0 %gather_fusion = bf16[160,256,256]{2,1,0:T(8,128)(2,1)} fusion(bf16[64,256,256]{2,1,0:T(8,128)(2,1)} %all-gather.3.cloned.1.call-done, s32[1024]{0:T(1024)S(1)} %pad_clamp_fusion.1), kind=kCustom, calls=%fused_computation | custom fusion | bytes 41943680 | tf_op jit(solution)/shard_map/gather | solution.py:26
  192.9 30.3 %multiply_bitcast_fusion.1 = f32[160,256,256]{1,2,0:T(8,128)} fusion(f32[160]{0:T(256)S(1)} %compare_convert_fusion, bf16[160,256,256]{2,1,0:T(8,128)(2,1)} %gather_fusion, bf16[1,1,160,256,256]{4,3,2,1,0:T(8,128)(2,1)} %param.10), kind=kOutput, calls=%fused_computation.5 | convolution fusion | flops 5379194880 | bytes 83886720 | tf_op jit(solution)/shard_map/tab,tbf->taf/dot_general | solution.py:28
  223.2 41.6 %copy.17 = f32[160,256,256]{2,1,0:T(8,128)} copy(f32[160,256,256]{1,2,0:T(8,128)} %multiply_bitcast_fusion.1) | data formatting | bytes 83886080 | tf_op jit(solution)/shard_map/mul | solution.py:28
  265.0 56.7 %scatter_fusion = f32[8,256,256]{2,1,0:T(8,128)S(1)} fusion(f32[8,256,256]{2,1,0:T(8,128)S(1)} %broadcast_in_dim.4, s32[160]{0:T(256)S(1)} %bitcast.38, f32[160,256,256]{2,1,0:T(8,128)} %copy.17), kind=kCustom, calls=%fused_computation.2 | custom fusion | flops 10485760 | bytes 125829760 | tf_op jit(solution)/shard_map/scatter-add | solution.py:34
  321.7 42.3 %all-reduce.4 = bf16[2048,256]{1,0:T(8,128)(2,1)S(1)} all-reduce(f32[2048,256]{1,0:T(8,128)S(1)} %bitcast.32), channel_id=1, replica_groups=mesh['node'=32,'rep'=4] {'rep'}, use_global_device_ids=true, to_apply=%region_1.0 | all-reduce | flops 524288 | bytes 3145728 | tf_op jit(solution)/shard_map/psum | solution.py:38
  364.1 3.8 multiply_convert_fusion
  367.8 0.5 convolution_convert_fusion
  368.3 1.9 fusion.9
  370.3 0.2 reduce-scatter.2.cloned.1.call-start
  370.5 9.6 %gather_fusion.1 = bf16[160,256,256]{2,1,0:T(8,128)(2,1)} fusion(bf16[8,256,256]{2,1,0:T(8,128)(2,1)S(1)} %bitcast.33, s32[1024]{0:T(1024)S(1)} %pad_clamp_fusion), kind=kCustom, calls=%fused_computation.1 | custom fusion | bytes 41943680 | tf_op jit(solution)/shard_map/gather | solution.py:55
  380.1 26.6 %multiply_bitcast_fusion = f32[160,256,256]{1,2,0:T(8,128)} fusion(f32[160]{0:T(256)S(1)} %compare_convert_fusion, bf16[160,256,256]{2,1,0:T(8,128)(2,1)} %gather_fusion.1, bf16[1,1,160,256,256]{4,3,2,1,0:T(8,128)(2,1)} %param.10), kind=kOutput, calls=%fused_computation.4 | convolution fusion | flops 5379194880 | bytes 83886720 | tf_op jit(solution)/shard_map/tab,taf->tbf/dot_general | solution.py:54
  406.7 41.7 %copy.19 = f32[160,256,256]{2,1,0:T(8,128)} copy(f32[160,256,256]{1,2,0:T(8,128)} %multiply_bitcast_fusion) | data formatting | bytes 83886080 | tf_op jit(solution)/shard_map/mul | solution.py:54
  448.3 7.8 %broadcast_in_dim.5 = f32[64,256,256]{2,1,0:T(8,128)} broadcast(f32[]{:T(128)} %constant.10.clone.1), dimensions={} | broadcast | bytes 16777220 | tf_op jit(solution)/shard_map/broadcast_in_dim | solution.py:60
  456.1 91.3 %scatter_fusion.1 = f32[64,256,256]{2,1,0:T(8,128)} fusion(f32[64,256,256]{2,1,0:T(8,128)} %broadcast_in_dim.5, s32[160]{0:T(256)S(1)} %bitcast.36, f32[160,256,256]{2,1,0:T(8,128)} %copy.19), kind=kCustom, calls=%fused_computation.3 | custom fusion | flops 10485760 | bytes 125829760 | tf_op jit(solution)/shard_map/scatter-add | solution.py:60
  547.5 1.8 fusion.8
  549.3 1.7 broadcast_multiply_fusion
  550.9 201.3 %reduce-scatter.2.cloned.1.call-done = f32[2,256,256]{2,1,0:T(8,128)} async-done(((f32[64,256,256]{2,1,0:T(8,128)}), f32[2,256,256]{2,1,0:T(8,128)}) %reduce-scatter.2.cloned.1.call-update) | async-done | bytes 524304 | tf_op jit(solution)/shard_map/reduce_scatter | solution.py:62
  752.3 1.8 convert_element_type.34
  (23 shorter events, 0.4 us)
Async XLA Ops:
  7.2 1.2 copy-start
  7.2 172.7 %all-gather.3.cloned.1.call-start = ((), (), s32[]{:S(2)}) async-start(), calls=%async_computation.1 | async-start | bytes 8650752 | tf_op jit(solution)/shard_map/all_gather | solution.py:25
  9.1 354.9 %all-gather.5.cloned.1.call-start = ((), (), s32[]{:S(2)}) async-start(), calls=%async_computation.2 | async-start | bytes 1310720 | tf_op jit(solution)/shard_map/all_gather | solution.py:39
  9.9 539.4 %all-reduce.3.cloned.1.call-start = ((), (), s32[]{:S(2)}) async-start(), calls=%async_computation.4 | async-start | bytes 524288 | tf_op jit(solution)/shard_map/psum | solution.py:51
  10.6 182.3 %copy-start.4 = (s32[160,1]{0,1:T(1,128)}, s32[160,1]{0,1:T(1,128)S(1)}, u32[]{:S(2)}) copy-start(s32[160,1]{0,1:T(1,128)S(1)} %compare_select_fusion) | copy-start | bytes 1924
  265.0 99.0 %copy-start.3 = (bf16[256,256]{1,0:T(8,128)(2,1)S(1)}, bf16[256,256]{1,0:T(8,128)(2,1)}, u32[]{:S(2)}) copy-start(bf16[256,256]{1,0:T(8,128)(2,1)} %param.8) | copy-start | bytes 393220
  364.0 3.8 copy-start.2
  370.3 382.0 %reduce-scatter.2.cloned.1.call-start = ((), (), s32[]{:S(2)}) async-start(), calls=%async_computation.3 | async-start | bytes 17301504 | tf_op jit(solution)/shard_map/reduce_scatter | solution.py:62
  406.7 49.5 %copy-start.5 = (s32[160,1]{0,1:T(1,128)S(1)}, s32[160,1]{0,1:T(1,128)}, u32[]{:S(2)}) copy-start(s32[160,1]{0,1:T(1,128)} %copy-done.4) | copy-start | bytes 1924
  456.1 297.9 %copy-start.1 = (bf16[2048,256]{1,0:T(8,128)(2,1)S(1)}, bf16[2048,256]{1,0:T(8,128)(2,1)}, u32[]{:S(2)}) copy-start(bf16[2048,256]{1,0:T(8,128)(2,1)} %param.7) | copy-start | bytes 3145732
Sparse Core Ops, SparseCore 0:
  10.2 169.6 all-gather.2
  181.6 21.7 all-gather.4
  370.4 142.5 all-reduce.2
  547.6 204.6 reduce-scatter.1
where the time goes:
time: 763 us; the launch traced here: 761 us
  waiting for transfers between devices  370 us (48%)
  other arithmetic  155 us (20%)
  local copies, waits for them, and re-layouts  116 us (15%)
  matrix products  63 us (8%)
  blocking collectives  42.3 us (6%)
  between operations  14.5 us (2%)
    reduce_scatter x1, waiting for transfers between devices, body(): lax.psum_scatter(column_part, 'node', scatter_dimension=0, tiled=True)  201 us
    all_gather x1, waiting for transfers between devices, body(): compact = lax.all_gather(mine, 'node', axis=0, tiled=True)  168 us
    scatter-add x1, other arithmetic, body(): jnp.zeros((compact_cols, block, feat), jnp.float32).at[slot_cols]  91.3 us
    scatter-add x1, other arithmetic, body(): partial_agg = jnp.zeros((row_blocks, block, feat), jnp.float32).at[slot_r...  56.7 us
    psum x1, blocking collectives, body(): aggregated = lax.psum(partial_agg, 'rep').astype(jnp.bfloat16)  42.3 us
    mul x1, local copies, waits for them, and re-layouts, body(): jnp.einsum('tab,taf->tbf', slot_tiles, dagg_blocks[slot_rows], preferred_...  41.7 us
    mul x1, local copies, waits for them, and re-layouts, body(): jnp.einsum('tab,tbf->taf', slot_tiles, picked, preferred_element_type=jnp...  41.6 us
    dot_general x1, matrix products, body(): jnp.einsum('tab,tbf->taf', slot_tiles, picked, preferred_element_type=jnp...  30.3 us
  transfers between devices with their start and end apart: 4, of which 2 were waited for; matrix products, arithmetic and copies ran while one was open for 43% of the time, Pallas kernels for 0%

commit v1 on v0

--- a/solution.py
+++ b/solution.py
@@ -2,6 +2,11 @@
 import jax.numpy as jnp
 from jax import lax
 from jax.sharding import PartitionSpec as P
+
+
+def summed_here(x, axis):
+    parts = lax.all_gather(x, axis)
+    return jnp.sum(parts, axis=0)
 
 
 def body(node_feats, weight, cotangent, tiles, tile_rows, tile_cols, tile_count):
@@ -35,7 +40,7 @@
         .reshape(rows, feat)
     )
     scale = float(rows * nnode) ** (-0.5)
-    aggregated = lax.psum(partial_agg, "rep").astype(jnp.bfloat16)
+    aggregated = summed_here(partial_agg, "rep").astype(jnp.bfloat16)
     cot_full = lax.all_gather(cotangent, "rep", axis=0, tiled=True)
     pre = jnp.dot(aggregated, weight, preferred_element_type=jnp.float32)
     sig = jax.nn.sigmoid(pre)

time: 763 us -> 805 us (1.055)
  waiting for transfers between devices: 370 us -> 449 us
  blocking collectives: 42.3 us -> 0 us
    all_gather x0 -> x1, waiting for transfers between devices: none -> 62.5 us  [summed_here(): parts = lax.all_gather(x, axis)]
    psum x1 -> x0, blocking collectives: 42.3 us -> none  [body(): aggregated = lax.psum(partial_agg, 'rep').astype(jnp.bfloat16)]
    all_gather x1, waiting for transfers between devices: 0.02 us -> 17.6 us  [body(): cot_full = lax.all_gather(cotangent, 'rep', axis=0, tiled=True)]
  transfers between devices with their start and end apart: 4 -> 5, of which waited for: 2 -> 4; matrix products, arithmetic and copies ran while one was open for 43% -> 23% of each run, Pallas kernels for 0% -> 0%
where the time goes in v1:
time: 805 us; the launch traced here: 803 us
  waiting for transfers between devices  449 us (56%)
  other arithmetic  159 us (20%)
  local copies, waits for them, and re-layouts  117 us (15%)
  matrix products  62.4 us (8%)
  between operations  14.5 us (2%)
    reduce_scatter x1, waiting for transfers between devices, body(): lax.psum_scatter(column_part, 'node', scatter_dimension=0, tiled=True)  200 us
    all_gather x1, waiting for transfers between devices, body(): compact = lax.all_gather(mine, 'node', axis=0, tiled=True)  169 us
    scatter-add x1, other arithmetic, body(): jnp.zeros((compact_cols, block, feat), jnp.float32).at[slot_cols]  91.1 us
    all_gather x1, waiting for transfers between devices, summed_here(): parts = lax.all_gather(x, axis)  62.5 us
    scatter-add x1, other arithmetic, body(): partial_agg = jnp.zeros((row_blocks, block, feat), jnp.float32).at[slot_r...  56.7 us
    mul x1, local copies, waits for them, and re-layouts, body(): jnp.einsum('tab,taf->tbf', slot_tiles, dagg_blocks[slot_rows], preferred_...  41.7 us
    mul x1, local copies, waits for them, and re-layouts, body(): jnp.einsum('tab,tbf->taf', slot_tiles, picked, preferred_element_type=jnp...  41.6 us
    dot_general x1, matrix products, body(): jnp.einsum('tab,tbf->taf', slot_tiles, picked, preferred_element_type=jnp...  30.3 us
  transfers between devices with their start and end apart: 5, of which 4 were waited for; matrix products, arithmetic and copies ran while one was open for 23% of the time, Pallas kernels for 0%

profile of v1, /device:TPU:0, one launch (start us, length us, event | category | flops | bytes accessed | tf_op | source)
XLA Modules:
  0.0 802.6 jit_solution(8371043184359536447)
XLA Ops:
  7.2 1.2 copy-done
  8.4 0.7 constant_dynamic-slice_fusion
  9.8 0.7 compare_select_fusion
  10.5 0.7 compare_select_fusion.1
  11.2 168.7 %all-gather.4.cloned.1.call-done = bf16[64,256,256]{2,1,0:T(8,128)(2,1)} async-done(((bf16[2,256,256]{2,1,0:T(8,128)(2,1)}), bf16[64,256,256]{2,1,0:T(8,128)(2,1)}) %all-gather.4.cloned.1.call-update) | async-done | bytes 8388624 | tf_op jit(solution)/shard_map/all_gather | solution.py:30
  179.9 13.0 %gather_fusion = bf16[160,256,256]{2,1,0:T(8,128)(2,1)} fusion(bf16[64,256,256]{2,1,0:T(8,128)(2,1)} %all-gather.4.cloned.1.call-done, s32[1024]{0:T(1024)S(1)} %pad_clamp_fusion.1), kind=kCustom, calls=%fused_computation | custom fusion | bytes 41943680 | tf_op jit(solution)/shard_map/gather | solution.py:31
  192.9 30.3 %multiply_bitcast_fusion.1 = f32[160,256,256]{1,2,0:T(8,128)} fusion(f32[160]{0:T(256)S(1)} %compare_convert_fusion, bf16[160,256,256]{2,1,0:T(8,128)(2,1)} %gather_fusion, bf16[1,1,160,256,256]{4,3,2,1,0:T(8,128)(2,1)} %param.10), kind=kOutput, calls=%fused_computation.5 | convolution fusion | flops 5379194880 | bytes 83886720 | tf_op jit(solution)/shard_map/tab,tbf->taf/dot_general | solution.py:33
  223.2 41.6 %copy.17 = f32[160,256,256]{2,1,0:T(8,128)} copy(f32[160,256,256]{1,2,0:T(8,128)} %multiply_bitcast_fusion.1) | data formatting | bytes 83886080 | tf_op jit(solution)/shard_map/mul | solution.py:33
  265.0 56.7 %scatter_fusion = f32[8,256,256]{2,1,0:T(8,128)S(1)} fusion(f32[8,256,256]{2,1,0:T(8,128)S(1)} %broadcast_in_dim.4, s32[160]{0:T(256)S(1)} %bitcast.37, f32[160,256,256]{2,1,0:T(8,128)} %copy.17), kind=kCustom, calls=%fused_computation.2 | custom fusion | flops 10485760 | bytes 125829760 | tf_op jit(solution)/shard_map/scatter-add | solution.py:39
  321.7 1.3 copy-done.2
  323.9 62.5 %all-gather.6.cloned.1.call-done = f32[4,2048,256]{2,1,0:T(8,128)} async-done(((f32[1,2048,256]{2,1,0:T(8,128)}), f32[4,2048,256]{2,1,0:T(8,128)}) %all-gather.6.cloned.1.call-update) | async-done | bytes 8388624 | tf_op jit(solution)/shard_map/all_gather | solution.py:8
  386.4 4.2 reduce_sum.9
  390.6 17.6 %all-gather.8.cloned.1.call-done = bf16[2048,256]{1,0:T(8,128)(2,1)} async-done(((bf16[512,256]{1,0:T(8,128)(2,1)}), bf16[2048,256]{1,0:T(8,128)(2,1)}) %all-gather.8.cloned.1.call-update) | async-done | bytes 1048592 | tf_op jit(solution)/shard_map/all_gather | solution.py:44
  408.3 4.0 multiply_convert_fusion
  412.8 1.0 fusion.9
  414.0 9.6 %gather_fusion.1 = bf16[160,256,256]{2,1,0:T(8,128)(2,1)} fusion(bf16[8,256,256]{2,1,0:T(8,128)(2,1)S(1)} %bitcast.33, s32[1024]{0:T(1024)S(1)} %pad_clamp_fusion), kind=kCustom, calls=%fused_computation.1 | custom fusion | bytes 41943680 | tf_op jit(solution)/shard_map/gather | solution.py:60
  423.6 26.6 %multiply_bitcast_fusion = f32[160,256,256]{1,2,0:T(8,128)} fusion(f32[160]{0:T(256)S(1)} %compare_convert_fusion, bf16[160,256,256]{2,1,0:T(8,128)(2,1)} %gather_fusion.1, bf16[1,1,160,256,256]{4,3,2,1,0:T(8,128)(2,1)} %param.10), kind=kOutput, calls=%fused_computation.4 | convolution fusion | flops 5379194880 | bytes 83886720 | tf_op jit(solution)/shard_map/tab,taf->tbf/dot_general | solution.py:59
  450.3 41.7 %copy.19 = f32[160,256,256]{2,1,0:T(8,128)} copy(f32[160,256,256]{1,2,0:T(8,128)} %multiply_bitcast_fusion) | data formatting | bytes 83886080 | tf_op jit(solution)/shard_map/mul | solution.py:59
  491.9 7.8 broadcast_in_dim.5
  499.7 91.1 %scatter_fusion.1 = f32[64,256,256]{2,1,0:T(8,128)} fusion(f32[64,256,256]{2,1,0:T(8,128)} %broadcast_in_dim.5, s32[160]{0:T(256)S(1)} %bitcast.36, f32[160,256,256]{2,1,0:T(8,128)} %copy.19), kind=kCustom, calls=%fused_computation.3 | custom fusion | flops 10485760 | bytes 125829760 | tf_op jit(solution)/shard_map/scatter-add | solution.py:65
  590.9 2.0 fusion.8
  592.9 1.7 broadcast_multiply_fusion
  594.5 199.8 %reduce-scatter.2.cloned.1.call-done = f32[2,256,256]{2,1,0:T(8,128)} async-done(((f32[64,256,256]{2,1,0:T(8,128)}), f32[2,256,256]{2,1,0:T(8,128)}) %reduce-scatter.2.cloned.1.call-update) | async-done | bytes 524304 | tf_op jit(solution)/shard_map/reduce_scatter | solution.py:67
  794.3 1.8 convert_element_type.34
  (26 shorter events, 1.8 us)
Async XLA Ops:
  7.2 1.2 copy-start
  7.2 172.7 %all-gather.4.cloned.1.call-start = ((), (), s32[]{:S(2)}) async-start(), calls=%async_computation.1 | async-start | bytes 8650752 | tf_op jit(solution)/shard_map/all_gather | solution.py:30
  9.1 377.2 %all-gather.6.cloned.1.call-start = ((), (), s32[]{:S(2)}) async-start(), calls=%async_computation.2 | async-start | bytes 10485760 | tf_op jit(solution)/shard_map/all_gather | solution.py:8
  10.5 182.3 %copy-start.4 = (s32[160,1]{0,1:T(1,128)}, s32[160,1]{0,1:T(1,128)S(1)}, u32[]{:S(2)}) copy-start(s32[160,1]{0,1:T(1,128)S(1)} %compare_select_fusion) | copy-start | bytes 1924
  265.0 143.3 %copy-start.3 = (bf16[256,256]{1,0:T(8,128)(2,1)S(1)}, bf16[256,256]{1,0:T(8,128)(2,1)}, u32[]{:S(2)}) copy-start(bf16[256,256]{1,0:T(8,128)(2,1)} %param.8) | copy-start | bytes 393220
  321.7 1.4 copy-start.2
  323.1 85.2 %all-gather.8.cloned.1.call-start = ((), (), s32[]{:S(2)}) async-start(), calls=%async_computation.3 | async-start | bytes 1310720 | tf_op jit(solution)/shard_map/all_gather | solution.py:44
  323.8 269.1 %all-reduce.2.cloned.1.call-start = ((), (), s32[]{:S(2)}) async-start(), calls=%async_computation.5 | async-start | bytes 524288 | tf_op jit(solution)/shard_map/psum | solution.py:56
  413.8 380.5 %reduce-scatter.2.cloned.1.call-start = ((), (), s32[]{:S(2)}) async-start(), calls=%async_computation.4 | async-start | bytes 17301504 | tf_op jit(solution)/shard_map/reduce_scatter | solution.py:67
  450.3 49.5 %copy-start.5 = (s32[160,1]{0,1:T(1,128)S(1)}, s32[160,1]{0,1:T(1,128)}, u32[]{:S(2)}) copy-start(s32[160,1]{0,1:T(1,128)} %copy-done.4) | copy-start | bytes 1924
  499.7 296.4 %copy-start.1 = (bf16[2048,256]{1,0:T(8,128)(2,1)S(1)}, bf16[2048,256]{1,0:T(8,128)(2,1)}, u32[]{:S(2)}) copy-start(bf16[2048,256]{1,0:T(8,128)(2,1)} %param.7) | copy-start | bytes 3145732
Sparse Core Ops, SparseCore 0:
  10.2 169.6 all-gather.3
  323.2 63.1 all-gather.5
  388.1 20.1 all-gather.7
  413.9 141.3 all-reduce.1
  591.0 203.2 reduce-scatter.1
